TPU v7x, 256 devices: a whole 4x4x8 slice. The times are simulated.
256 devices in a mesh: gx: 32 (over x_hi, z, core), gy: 8 (over x_lo, y).
Axes of the slice: x: 4 (x_hi: 2, x_lo: 2; x = x_hi * 2 + x_lo), y: 4, z: 8, core: 2. Of those that a mesh axis runs over, the one named last changes fastest.
Arguments:
- background: bfloat16 [2, 2048, 1024, 128], P(None, 'gx', 'gy'), may hold values from -6 to 6
- observation_cell_index: int32 [32, 8, 512], P('gx', 'gy'), may hold values from 0 to 16383
- obs_value: float32 [32, 8, 512], P('gx', 'gy'), may hold values from -6 to 6
- obs_inverse: float32 [32, 8, 512], P('gx', 'gy'), may hold values from 0.5 to 4
- obs_count: int32 [32, 8], P('gx', 'gy'), may hold values from 256 to 512, as said below
- taper: int32 [64], replicated, may hold values from 32 to 1024
Outputs:
- analysis: bfloat16 [2, 2048, 1024, 128], P(None, 'gx', 'gy')
Inputs may be any that keep to these rules, and one draw needn't show every extreme that they name: `obs_count`: some tile has exactly 512 live slots and some tile exactly 256.
All inputs are finite; a program needn't handle non-finite values.
Results may differ from a plain program's by a relative error of at most 0.0028.
The roundings to bfloat16 on the way count: a program that leaves them out, or rounds other values in their place, can miss the bound.
Values may be sent and summed in bfloat16 or wider, within the bound.
A program may use at most 64 MiB of HBM per device.

v0:
```python
import jax
import jax.numpy as jnp
from jax import lax
from jax.sharding import PartitionSpec as P

NSTEPS = 6


HIGH = lax.Precision.HIGHEST


def extended(cells, sides, width):
    for axis, dim in sides:
        count = lax.axis_size(axis)
        ends = count - 1
        head = lax.slice_in_dim(cells, 0, width, axis=dim)
        tail = lax.slice_in_dim(cells, cells.shape[dim] - width, cells.shape[dim], axis=dim)
        cells = jnp.concatenate(
            [
                lax.ppermute(tail, axis, [(i, (i + 1) % count) for i in range(ends)]),
                cells,
                lax.ppermute(head, axis, [((i + 1) % count, i) for i in range(ends)]),
            ],
            axis=dim,
        )
    return cells


def observe(ensemble, cell_ids, values, inverse, live_count, tile_x, tile_y):
    picked = jnp.take(ensemble, cell_ids, axis=0).astype(jnp.float32)
    center = jnp.mean(picked, axis=1)
    perturb = (picked - center[:, None]).astype(jnp.bfloat16)
    slot_ids = jnp.arange(cell_ids.shape[0], dtype=jnp.int32)
    live_mask = (slot_ids < live_count).astype(jnp.float32)
    column_pos = cell_ids % (tile_x * tile_y) // tile_y
    row_pos = cell_ids % tile_y
    metadata = jnp.stack(
        [
            values - center,
            inverse * live_mask,
            column_pos.astype(jnp.float32),
            row_pos.astype(jnp.float32),
        ]
    ).astype(jnp.bfloat16)
    return (perturb, metadata, live_mask)


def statistics(perturb, metadata, live_mask):
    members = perturb.shape[1]
    weight = metadata[1].astype(jnp.float32)
    innovation = metadata[0].astype(jnp.float32)
    spread = jnp.sum(jnp.square(perturb.astype(jnp.float32)), axis=1) / (members - 1)
    return (
        jnp.sum(weight * innovation * innovation),
        jnp.sum(weight * spread) + jnp.sum(live_mask),
    )


def transform(perturb9, metadata9, inflation, taper, tile_x, tile_y):
    members = perturb9.shape[-1]
    bins = taper.shape[0]
    offsets = jnp.arange(3, dtype=jnp.int32) - 1
    column_pos = offsets[:, None, None] * tile_x + metadata9[:, :, 2, :].astype(jnp.int32)
    row_pos = offsets[None, :, None] * tile_y + metadata9[:, :, 3, :].astype(jnp.int32)
    delta_x = 2 * column_pos - (tile_x - 1)
    delta_y = 2 * row_pos - (tile_y - 1)
    distance = (delta_x * delta_x + delta_y * delta_y) * bins
    limit = 9 * (tile_x * tile_x + tile_y * tile_y)
    bin_edges = jnp.arange(bins, dtype=jnp.int32) * limit
    in_bin = (distance[..., None] >= bin_edges) & (distance[..., None] < bin_edges + limit)
    tapered_weight_factor = (
        jnp.sum(jnp.where(in_bin, taper.astype(jnp.float32), jnp.float32(0.0)), axis=-1) / 1024.0
    )
    effective = metadata9[:, :, 1, :].astype(jnp.float32) * tapered_weight_factor
    flat = perturb9.reshape(-1, members)
    weighted = (flat.astype(jnp.float32) * effective.reshape(-1)[:, None]).astype(jnp.bfloat16)
    gram_matrix = lax.dot_general(
        weighted, flat, (((0,), (0,)), ((), ())), preferred_element_type=jnp.float32
    )
    innovation = metadata9[:, :, 0, :].reshape(1, -1)
    projected = jnp.dot(innovation, weighted, preferred_element_type=jnp.float32)[0]
    identity = jnp.eye(members, dtype=jnp.float32)
    system = identity / inflation + gram_matrix / (members - 1)
    frobenius = jnp.sqrt(jnp.sum(system * system))
    root_iter = system / frobenius
    inverse_root = identity
    for sweep in range(NSTEPS):
        correction = 1.5 * identity - 0.5 * jnp.dot(
            inverse_root, root_iter, precision=HIGH, preferred_element_type=jnp.float32
        )
        root_iter = jnp.dot(
            root_iter, correction, precision=HIGH, preferred_element_type=jnp.float32
        )
        inverse_root = jnp.dot(
            correction, inverse_root, precision=HIGH, preferred_element_type=jnp.float32
        )
    spread_weights = inverse_root / jnp.sqrt(frobenius)
    inner = jnp.dot(inverse_root, projected, precision=HIGH, preferred_element_type=jnp.float32)
    mean_weights = jnp.dot(
        inverse_root, inner, precision=HIGH, preferred_element_type=jnp.float32
    ) / (frobenius * (members - 1))
    return (spread_weights + mean_weights[:, None]).astype(jnp.bfloat16)


def spline(length, tile_id, tiles):
    position = (jnp.arange(length, dtype=jnp.float32) + 0.5) / length
    left_part = 0.5 * jnp.square(1.0 - position)
    middle = 0.5 + position - jnp.square(position)
    right_part = 0.5 * jnp.square(position)
    has_left = (tile_id > 0).astype(jnp.float32)
    has_right = (tile_id < tiles - 1).astype(jnp.float32)
    middle = middle + (1.0 - has_left) * left_part + (1.0 - has_right) * right_part
    return jnp.stack([left_part * has_left, middle, right_part * has_right])


def blend(ensemble, weights9, column_id, row_id, columns, row_tiles):
    levels, tile_x, tile_y, members = ensemble.shape
    widened = ensemble.astype(jnp.float32)
    center = jnp.mean(widened, axis=-1, keepdims=True)
    deviation = widened - center
    beta_x = spline(tile_x, column_id, columns)
    beta_y = spline(tile_y, row_id, row_tiles)
    analysis = center
    for offset_y in range(3):
        pieces = [
            (
                deviation
                * (beta_x[offset_x][:, None] * beta_y[offset_y][None, :])[None, :, :, None]
            ).astype(jnp.bfloat16)
            for offset_x in range(3)
        ]
        stacked = jnp.concatenate(pieces, axis=-1).reshape(-1, 3 * members)
        column_stack = weights9[:, offset_y].reshape(3 * members, members)
        product = jnp.dot(stacked, column_stack, preferred_element_type=jnp.float32)
        analysis = analysis + product.reshape(levels, tile_x, tile_y, members)
    return analysis.astype(jnp.bfloat16)


def local(background, observation_cell_index, obs_value, obs_inverse, obs_count, taper):
    levels, tile_x, tile_y, members = background.shape
    slot_total = observation_cell_index.shape[2]
    ensemble = background.reshape(-1, members)
    perturb, metadata, live_mask = observe(
        ensemble,
        observation_cell_index[0, 0],
        obs_value[0, 0],
        obs_inverse[0, 0],
        obs_count[0, 0],
        tile_x,
        tile_y,
    )
    numerator, denominator = statistics(perturb, metadata, live_mask)
    numerator, denominator = lax.psum((numerator, denominator), ("gx", "gy"))
    inflation = numerator / denominator
    packed = jnp.concatenate([perturb, metadata.reshape(-1, members)], axis=0)[None, None]
    adjacent_tiles = extended(packed, (("gx", 0), ("gy", 1)), 1)
    neighbour_perturbation_rows = adjacent_tiles[:, :, :slot_total]
    neighbour_metadata_rows = adjacent_tiles[:, :, slot_total:].reshape(3, 3, 4, slot_total)
    tile_weights = transform(
        neighbour_perturbation_rows, neighbour_metadata_rows, inflation, taper, tile_x, tile_y
    )[None, None]
    near_weights = extended(tile_weights, (("gx", 0), ("gy", 1)), 1)
    return blend(
        background,
        near_weights,
        lax.axis_index("gx"),
        lax.axis_index("gy"),
        lax.axis_size("gx"),
        lax.axis_size("gy"),
    )


def solution(mesh):
    in_specs = (
        P(None, "gx", "gy", None),
        P("gx", "gy", None),
        P("gx", "gy", None),
        P("gx", "gy", None),
        P("gx", "gy"),
        P(),
    )
    out_specs = P(None, "gx", "gy", None)
    return jax.shard_map(local, mesh=mesh, in_specs=in_specs, out_specs=out_specs, check_vma=False)
```

profile of v0, /device:TPU:6, one launch (start us, length us, event | category | flops | bytes accessed | tf_op | source)
XLA Modules:
  0.0 183.8 jit_solution(1450910014959891026)
XLA Ops:
  0.0 0.7 fusion.60
  0.7 0.7 compare_select_fusion
  2.1 0.7 compare_and_fusion
  2.8 3.8 %gather_fusion = bf16[512,128]{1,0:T(8,128)(2,1)S(1)} fusion(bf16[16384,128]{1,0:T(8,128)(2,1)} %bitcast.130, s32[1024]{0:T(1024)S(1)} %pad_clamp_fusion), kind=kCustom, calls=%fused_computation | custom fusion | bytes 264192 | tf_op jit(solution)/shard_map/jit(_take)/gather | solution.py:30
  6.6 0.2 convert_reduce_fusion.1
  6.8 0.3 multiply_reduce_fusion
  7.1 0.7 compare_select_fusion.1
  7.9 8.0 %collective-permute-start.1 = (bf16[1,1,528,128]{3,2,1,0:T(8,128)(2,1)S(1)}, bf16[1,1,528,128]{3,2,1,0:T(8,128)(2,1)S(1)}, u32[]{:S(2)}, u32[]{:S(2)}) collective-permute-start(bf16[1,1,528,128]{3,2,1,0:T(8,128)(2,1)S(1)} %maximum_bitcast_fusion), channel_id=1, source_target_pairs={{8,0},{16,8},{24,16},{32,24},{40,32},{48,40},{56,48},{64,56},{72,6... | collective-permute-start | bytes 405512 | tf_op jit(solution)/shard_map/ppermute | solution.py:22
  15.9 1.9 %collective-permute-start = (bf16[1,1,528,128]{3,2,1,0:T(8,128)(2,1)S(1)}, bf16[1,1,528,128]{3,2,1,0:T(8,128)(2,1)S(1)}, u32[]{:S(2)}, u32[]{:S(2)}) collective-permute-start(bf16[1,1,528,128]{3,2,1,0:T(8,128)(2,1)S(1)} %maximum_bitcast_fusion), channel_id=1, source_target_pairs={{0,8},{8,16},{16,24},{24,32},{32,40},{40,48},{48,56},{56,64},{64,7... | collective-permute-start | bytes 405512 | tf_op jit(solution)/shard_map/ppermute | solution.py:20
  17.9 3.4 %convert_reduce_fusion = f32[2,64,128]{2,1,0:T(8,128)S(1)} fusion(bf16[2,64,128,128]{3,2,1,0:T(8,128)(2,1)} %param.6), kind=kLoop, calls=%fused_computation.20 | loop fusion | flops 4177920 | bytes 4259840 | tf_op jit(solution)/shard_map/reduce_sum | solution.py:119
  21.3 0.7 fusion.58
  22.0 0.6 convert_reduce_fusion.2
  23.8 77.6 %all-reduce = (f32[]{:T(128)}, f32[]{:T(128)}) all-reduce(f32[]{:T(128)S(6)} %add.238, f32[]{:T(128)} %get-tuple-element.5), channel_id=1, replica_groups=mesh['gx'=32,'gy'=8] {'gx','gy'}, use_global_device_ids=true, to_apply=%region_5.6 | all-reduce | flops 2 | bytes 16 | tf_op jit(solution)/shard_map/psum | solution.py:153
  102.7 2.8 %collective-permute-start.3 = (bf16[3,1,528,128]{3,2,1,0:T(8,128)(2,1)S(1)}, bf16[3,1,528,128]{3,2,1,0:T(8,128)(2,1)S(1)}, u32[]{:S(2)}, u32[]{:S(2)}) collective-permute-start(bf16[3,1,528,128]{3,2,1,0:T(8,128)(2,1)S(1)} %pad_maximum_fusion.1), channel_id=1, source_target_pairs={{1,0},{2,1},{3,2},{4,3},{5,4},{6,5},{7,6},{9,8},{10,9},{11,10},{12... | collective-permute-start | bytes 1216520 | tf_op jit(solution)/shard_map/ppermute | solution.py:22
  105.5 3.1 %collective-permute-start.2 = (bf16[3,1,528,128]{3,2,1,0:T(8,128)(2,1)S(1)}, bf16[3,1,528,128]{3,2,1,0:T(8,128)(2,1)S(1)}, u32[]{:S(2)}, u32[]{:S(2)}) collective-permute-start(bf16[3,1,528,128]{3,2,1,0:T(8,128)(2,1)S(1)} %pad_maximum_fusion.1), channel_id=1, source_target_pairs={{0,1},{1,2},{2,3},{3,4},{4,5},{5,6},{6,7},{8,9},{9,10},{10,11},{11... | collective-permute-start | bytes 1216520 | tf_op jit(solution)/shard_map/ppermute | solution.py:20
  108.7 7.0 %collective-permute-done.3 = bf16[3,1,528,128]{3,2,1,0:T(8,128)(2,1)S(1)} collective-permute-done((bf16[3,1,528,128]{3,2,1,0:T(8,128)(2,1)S(1)}, bf16[3,1,528,128]{3,2,1,0:T(8,128)(2,1)S(1)}, u32[]{:S(2)}, u32[]{:S(2)}) %collective-permute-start.3) | collective-permute-done | bytes 405536 | tf_op jit(solution)/shard_map/ppermute | solution.py:22
  115.7 4.6 %collective-permute-done.2 = bf16[3,1,528,128]{3,2,1,0:T(8,128)(2,1)S(1)} collective-permute-done((bf16[3,1,528,128]{3,2,1,0:T(8,128)(2,1)S(1)}, bf16[3,1,528,128]{3,2,1,0:T(8,128)(2,1)S(1)}, u32[]{:S(2)}, u32[]{:S(2)}) %collective-permute-start.2) | collective-permute-done | bytes 405536 | tf_op jit(solution)/shard_map/ppermute | solution.py:20
  120.6 0.3 select_reduce_fusion
  121.0 0.8 multiply_convert_fusion
  121.8 1.1 multiply_reduce_fusion.1
  123.6 0.2 fusion.41
  123.8 0.2 fusion.47
  124.0 0.2 fusion.49
  124.2 0.2 fusion.40
  124.4 0.2 fusion.72
  124.7 0.2 fusion.73
  124.9 0.2 fusion.39
  125.1 0.2 fusion.74
  125.3 0.2 fusion.75
  125.5 0.2 fusion.38
  125.7 0.2 fusion.76
  125.9 0.2 fusion.77
  126.1 0.2 fusion.37
  126.4 0.2 fusion.78
  126.6 0.2 fusion.79
  126.8 0.2 fusion.36
  127.0 0.2 fusion.80
  127.2 0.3 convolution_bitcast_fusion.3
  127.5 0.2 convolution_bitcast_fusion.2
  127.7 0.2 fusion.44
  128.1 2.8 %collective-permute-start.5 = (bf16[1,1,128,128]{3,2,1,0:T(8,128)(2,1)S(1)}, bf16[1,1,128,128]{3,2,1,0:T(8,128)(2,1)S(1)}, u32[]{:S(2)}, u32[]{:S(2)}) collective-permute-start(bf16[1,1,128,128]{3,2,1,0:T(8,128)(2,1)S(1)} %fusion.48), channel_id=1, source_target_pairs={{8,0},{16,8},{24,16},{32,24},{40,32},{48,40},{56,48},{64,56},{72,6... | collective-permute-start | bytes 98312 | tf_op jit(solution)/shard_map/ppermute | solution.py:22
  130.9 1.9 %collective-permute-start.4 = (bf16[1,1,128,128]{3,2,1,0:T(8,128)(2,1)S(1)}, bf16[1,1,128,128]{3,2,1,0:T(8,128)(2,1)S(1)}, u32[]{:S(2)}, u32[]{:S(2)}) collective-permute-start(bf16[1,1,128,128]{3,2,1,0:T(8,128)(2,1)S(1)} %fusion.48), channel_id=1, source_target_pairs={{0,8},{8,16},{16,24},{24,32},{32,40},{40,48},{48,56},{56,64},{64,7... | collective-permute-start | bytes 98312 | tf_op jit(solution)/shard_map/ppermute | solution.py:20
  132.8 17.4 %fusion.33 = (bf16[2,64,128,128]{3,2,1,0:T(8,128)(2,1)S(1)}, bf16[2,64,128,128]{3,2,1,0:T(8,128)(2,1)S(1)}, bf16[2,64,128,128]{3,2,1,0:T(8,128)(2,1)S(1)}, bf16[...) fusion(bf16[2,64,128,128]{3,2,1,0:T(8,128)(2,1)} %param.6, ...), kind=kLoop, calls=%fused_computation.36 | loop fusion | flops 41943040 | bytes 42303488 | tf_op jit(solution)/shard_map/convert_element_type | solution.py:129
  150.2 1.9 %collective-permute-start.6 = (bf16[3,1,128,128]{3,2,1,0:T(8,128)(2,1)S(1)}, bf16[3,1,128,128]{3,2,1,0:T(8,128)(2,1)S(1)}, u32[]{:S(2)}, u32[]{:S(2)}) collective-permute-start(bf16[3,1,128,128]{3,2,1,0:T(8,128)(2,1)S(1)} %pad_maximum_fusion.2), channel_id=1, source_target_pairs={{0,1},{1,2},{2,3},{3,4},{4,5},{5,6},{6,7},{8,9},{9,10},{10,11},{11... | collective-permute-start | bytes 294920 | tf_op jit(solution)/shard_map/ppermute | solution.py:20
  152.2 6.0 %collective-permute-start.7 = (bf16[3,1,128,128]{3,2,1,0:T(8,128)(2,1)S(1)}, bf16[3,1,128,128]{3,2,1,0:T(8,128)(2,1)S(1)}, u32[]{:S(2)}, u32[]{:S(2)}) collective-permute-start(bf16[3,1,128,128]{3,2,1,0:T(8,128)(2,1)S(1)} %pad_maximum_fusion.2), channel_id=1, source_target_pairs={{1,0},{2,1},{3,2},{4,3},{5,4},{6,5},{7,6},{9,8},{10,9},{11,10},{12... | collective-permute-start | bytes 294920 | tf_op jit(solution)/shard_map/ppermute | solution.py:22
  158.2 8.5 %fusion.6 = f32[2,64,128,128]{3,2,1,0:T(8,128)} fusion(bf16[384,128,1,1]{1,0,3,2:T(8,128)(2,1)S(1)} %bitcast.132, bf16[2,64,128,128]{3,2,1,0:T(8,128)(2,1)} %get-tuple-element.16, bf16[2,64,128,128]{3,2,1,0:T(8,128)(2,1)} %get-tuple-element.15, bf16[2,64,128,128]{3,2,1,0:T(8,128)(2,1)} %get-tuple-element.14), kind=kOutput, calls=%fused_computation.7 | convolution fusion | flops 1648361472 | bytes 21069824 | tf_op jit(solution)/shard_map/dot_general | solution.py:134
  166.7 5.7 %fusion = f32[2,64,128,128]{3,2,1,0:T(8,128)} fusion(bf16[384,128,1,1]{1,0,3,2:T(8,128)(2,1)S(1)} %bitcast.140, bf16[2,64,128,128]{3,2,1,0:T(8,128)(2,1)S(1)} %get-tuple-element.13, bf16[2,64,128,128]{3,2,1,0:T(8,128)(2,1)S(1)} %get-tuple-element.12, bf16[2,64,128,128]{3,2,1,0:T(8,128)(2,1)S(1)} %get-tuple-element.19), kind=kOutput, calls=%fused_computation.1 | convolution fusion | flops 1648361472 | bytes 21069824 | tf_op jit(solution)/shard_map/dot_general | solution.py:134
  172.4 11.4 %add_convert_fusion = bf16[2,64,128,128]{3,2,1,0:T(8,128)(2,1)} fusion(f32[2,64,128,128]{3,2,1,0:T(8,128)} %fusion.6, f32[2,64,128,128]{3,2,1,0:T(8,128)} %fusion, f32[2,64,128]{2,1,0:T(8,128)S(1)} %broadcast_multiply_fusion, bf16[384,128,1,1]{1,0,3,2:T(8,128)(2,1)S(1)} %bitcast.139, bf16[2,64,128,128]{3,2,1,0:T(8,128)(2,1)S(1)} %get-tuple-element.18, ...), kind=kOutput, calls=%fused_computation.39 | convolution fusion | flops 1656750080 | bytes 33718272 | tf_op jit(solution)/shard_map/dot_general | solution.py:134
  (32 shorter events, 0.8 us)
Async XLA Ops:
  0.0 101.4 %copy-start = (s32[64]{0:T(128)S(1)}, s32[64]{0:T(128)}, u32[]{:S(2)}) copy-start(s32[64]{0:T(128)} %param.11) | copy-start | bytes 772
  7.9 94.8 %collective-permute-start.1 = (bf16[1,1,528,128]{3,2,1,0:T(8,128)(2,1)S(1)}, bf16[1,1,528,128]{3,2,1,0:T(8,128)(2,1)S(1)}, u32[]{:S(2)}, u32[]{:S(2)}) collective-permute-start(bf16[1,1,528,128]{3,2,1,0:T(8,128)(2,1)S(1)} %maximum_bitcast_fusion), channel_id=1, source_target_pairs={{8,0},{16,8},{24,16},{32,24},{40,32},{48,40},{56,48},{64,56},{72,6... | collective-permute-start | bytes 405512 | tf_op jit(solution)/shard_map/ppermute | solution.py:22
  15.9 86.8 %collective-permute-start = (bf16[1,1,528,128]{3,2,1,0:T(8,128)(2,1)S(1)}, bf16[1,1,528,128]{3,2,1,0:T(8,128)(2,1)S(1)}, u32[]{:S(2)}, u32[]{:S(2)}) collective-permute-start(bf16[1,1,528,128]{3,2,1,0:T(8,128)(2,1)S(1)} %maximum_bitcast_fusion), channel_id=1, source_target_pairs={{0,8},{8,16},{16,24},{24,32},{32,40},{40,48},{48,56},{56,64},{64,7... | collective-permute-start | bytes 405512 | tf_op jit(solution)/shard_map/ppermute | solution.py:20
  102.7 13.0 %collective-permute-start.3 = (bf16[3,1,528,128]{3,2,1,0:T(8,128)(2,1)S(1)}, bf16[3,1,528,128]{3,2,1,0:T(8,128)(2,1)S(1)}, u32[]{:S(2)}, u32[]{:S(2)}) collective-permute-start(bf16[3,1,528,128]{3,2,1,0:T(8,128)(2,1)S(1)} %pad_maximum_fusion.1), channel_id=1, source_target_pairs={{1,0},{2,1},{3,2},{4,3},{5,4},{6,5},{7,6},{9,8},{10,9},{11,10},{12... | collective-permute-start | bytes 1216520 | tf_op jit(solution)/shard_map/ppermute | solution.py:22
  105.5 14.8 %collective-permute-start.2 = (bf16[3,1,528,128]{3,2,1,0:T(8,128)(2,1)S(1)}, bf16[3,1,528,128]{3,2,1,0:T(8,128)(2,1)S(1)}, u32[]{:S(2)}, u32[]{:S(2)}) collective-permute-start(bf16[3,1,528,128]{3,2,1,0:T(8,128)(2,1)S(1)} %pad_maximum_fusion.1), channel_id=1, source_target_pairs={{0,1},{1,2},{2,3},{3,4},{4,5},{5,6},{6,7},{8,9},{9,10},{10,11},{11... | collective-permute-start | bytes 1216520 | tf_op jit(solution)/shard_map/ppermute | solution.py:20
  128.1 22.1 %collective-permute-start.5 = (bf16[1,1,128,128]{3,2,1,0:T(8,128)(2,1)S(1)}, bf16[1,1,128,128]{3,2,1,0:T(8,128)(2,1)S(1)}, u32[]{:S(2)}, u32[]{:S(2)}) collective-permute-start(bf16[1,1,128,128]{3,2,1,0:T(8,128)(2,1)S(1)} %fusion.48), channel_id=1, source_target_pairs={{8,0},{16,8},{24,16},{32,24},{40,32},{48,40},{56,48},{64,56},{72,6... | collective-permute-start | bytes 98312 | tf_op jit(solution)/shard_map/ppermute | solution.py:22
  130.9 19.3 %collective-permute-start.4 = (bf16[1,1,128,128]{3,2,1,0:T(8,128)(2,1)S(1)}, bf16[1,1,128,128]{3,2,1,0:T(8,128)(2,1)S(1)}, u32[]{:S(2)}, u32[]{:S(2)}) collective-permute-start(bf16[1,1,128,128]{3,2,1,0:T(8,128)(2,1)S(1)} %fusion.48), channel_id=1, source_target_pairs={{0,8},{8,16},{16,24},{24,32},{32,40},{40,48},{48,56},{56,64},{64,7... | collective-permute-start | bytes 98312 | tf_op jit(solution)/shard_map/ppermute | solution.py:20
  150.2 16.5 %collective-permute-start.6 = (bf16[3,1,128,128]{3,2,1,0:T(8,128)(2,1)S(1)}, bf16[3,1,128,128]{3,2,1,0:T(8,128)(2,1)S(1)}, u32[]{:S(2)}, u32[]{:S(2)}) collective-permute-start(bf16[3,1,128,128]{3,2,1,0:T(8,128)(2,1)S(1)} %pad_maximum_fusion.2), channel_id=1, source_target_pairs={{0,1},{1,2},{2,3},{3,4},{4,5},{5,6},{6,7},{8,9},{9,10},{10,11},{11... | collective-permute-start | bytes 294920 | tf_op jit(solution)/shard_map/ppermute | solution.py:20
  152.2 20.2 %collective-permute-start.7 = (bf16[3,1,128,128]{3,2,1,0:T(8,128)(2,1)S(1)}, bf16[3,1,128,128]{3,2,1,0:T(8,128)(2,1)S(1)}, u32[]{:S(2)}, u32[]{:S(2)}) collective-permute-start(bf16[3,1,128,128]{3,2,1,0:T(8,128)(2,1)S(1)} %pad_maximum_fusion.2), channel_id=1, source_target_pairs={{1,0},{2,1},{3,2},{4,3},{5,4},{6,5},{7,6},{9,8},{10,9},{11,10},{12... | collective-permute-start | bytes 294920 | tf_op jit(solution)/shard_map/ppermute | solution.py:22
where the time goes:
time: 186 us; the launch traced here: 184 us
  blocking collectives  77.6 us (42%)
  matrix products  30.8 us (17%)
  starting transfers between devices  28.5 us (15%)
  other arithmetic  27.2 us (15%)
  waiting for transfers between devices  11.6 us (6%)
  between operations  4.26 us (2%)
  local copies, waits for them, and re-layouts  3.82 us (2%)
    psum x1, blocking collectives, local(): numerator, denominator = lax.psum((numerator, denominator), ('gx', 'gy'))  77.6 us
    dot_general x3, matrix products, blend(): product = jnp.dot(stacked, column_stack, preferred_element_type=jnp.float32)  25.6 us
    ppermute x4, starting transfers between devices, extended(): lax.ppermute(head, axis, [((i + 1) % count, i) for i in range(ends)])  19.7 us
    convert_element_type x1, other arithmetic, blend(): pieces = [(deviation * (beta_x[offset_x][:, None] * beta_y[offset_y][None...  17.4 us
    ppermute x4, starting transfers between devices, extended(): lax.ppermute(tail, axis, [(i, (i + 1) % count) for i in range(ends)])  8.84 us
    ppermute x4, waiting for transfers between devices, extended(): lax.ppermute(head, axis, [((i + 1) % count, i) for i in range(ends)])  7.03 us
    ppermute x4, waiting for transfers between devices, extended(): lax.ppermute(tail, axis, [(i, (i + 1) % count) for i in range(ends)])  4.61 us
    gather x1, local copies, waits for them, and re-layouts, observe(): picked = jnp.take(ensemble, cell_ids, axis=0).astype(jnp.float32)  3.78 us
  transfers between devices with their start and end apart: 8, of which 2 were waited for; matrix products, arithmetic and copies ran while one was open for 20% of the time, Pallas kernels for 0%

commit v1 on v0

v1 whole, which is shorter than its diff:
```python
import functools

import jax
import jax.numpy as jnp
from jax import lax
from jax.experimental import pallas as pl
from jax.experimental.pallas import tpu as pltpu
from jax.sharding import PartitionSpec as P

NSTEPS = 6
HIGH = lax.Precision.HIGHEST
MESH = pl.DeviceIdType.MESH
F32 = jnp.float32
BF16 = jnp.bfloat16

K = 128
OBS = 512
TX = 64
TY = 128
BINS = 64
LIMIT = 9 * (TX * TX + TY * TY)
CELLS = 2 * TX * TY
LOADS = 8
GROWS = K + 8
BLOCK = 16


def nt(a, b):
    return lax.dot_general(a, b, (((1,), (1,)), ((), ())), preferred_element_type=F32)


def mm(a, b):
    return jnp.dot(a, b, preferred_element_type=F32)


def high(a, b):
    return jnp.dot(a, b, precision=HIGH, preferred_element_type=F32)


def beta(position, has_low, has_high):
    low = 0.5 * ((1.0 - position) * (1.0 - position))
    middle = 0.5 + position - position * position
    top = 0.5 * (position * position)
    middle = middle + (1.0 - has_low) * low + (1.0 - has_high) * top
    return low * has_low, middle, top * has_high


def kernel(
    n_gx,
    n_gy,
    field,
    cell_s,
    cell_v,
    value,
    inverse,
    count,
    taper,
    out,
    field_v,
    acc,
    s_own,
    u_side,
    t_mid,
    t_ends,
    by_tab,
    picked,
    weighted,
    rhs,
    gram,
    gram_x,
    half,
    gram_y,
    sum_a,
    sum_b,
    w_all,
    load_sem,
    send_a,
    recv_a,
    send_b,
    recv_b,
    send_gx,
    recv_gx,
    send_gy,
    recv_gy,
    send_wy,
    recv_wy,
    send_wx,
    recv_wx,
    send_wc,
    recv_wc,
):
    gx = lax.axis_index("gx")
    gy = lax.axis_index("gy")
    span = CELLS // LOADS
    loads = [
        pltpu.make_async_copy(
            field.at[pl.ds(k * span, span), :], field_v.at[pl.ds(k * span, span), :], load_sem.at[k]
        )
        for k in range(LOADS)
    ]
    for load in loads:
        load.start()

    gram_x[...] = jnp.zeros_like(gram_x)
    gram_y[...] = jnp.zeros_like(gram_y)
    w_all[...] = jnp.zeros_like(w_all)

    block = lax.div(gx, BLOCK)
    lane = lax.rem(gx, BLOCK)
    plane = block * n_gy + gy
    planes = n_gx // BLOCK * n_gy

    def ring_peer(k):
        return (block * BLOCK + lax.rem(lane + k, BLOCK), gy)

    def plane_peer(k):
        other = lax.rem(plane + k, planes)
        return (lax.div(other, n_gy) * BLOCK + lane, lax.rem(other, n_gy))

    west, east = gx > 0, gx < n_gx - 1
    south, north = gy > 0, gy < n_gy - 1
    sides = [
        (west, (gx - 1, gy)),
        (east, (gx + 1, gy)),
        (south, (gx, gy - 1)),
        (north, (gx, gy + 1)),
    ]

    barrier = pltpu.get_barrier_semaphore()
    for k in range(1, BLOCK):
        pl.semaphore_signal(barrier, inc=1, device_id=ring_peer(k), device_id_type=MESH)
    for k in range(1, planes):
        pl.semaphore_signal(barrier, inc=1, device_id=plane_peer(k), device_id_type=MESH)
    for there, peer in sides:

        @pl.when(there)
        def _(peer=peer):
            pl.semaphore_signal(barrier, inc=1, device_id=peer, device_id_type=MESH)

    cells = cell_v[...]
    col = lax.shift_right_logical(cells & (TX * TY - 1), 7)
    row = cells & (TY - 1)
    slot = lax.broadcasted_iota(jnp.int32, (1, OBS), 1)
    live = (slot < count[0, 0]).astype(F32)
    weight = (inverse[...] * live).astype(BF16).astype(F32)
    which = lax.broadcasted_iota(jnp.int32, (BLOCK, OBS), 0)
    third = lax.shift_right_logical(which * 11, 5)
    dx = 2 * ((third - 1) * TX + col) - (TX - 1)
    dy = 2 * ((which - third * 3 - 1) * TY + row) - (TY - 1)
    distance = (dx * dx + dy * dy) * BINS
    factor = jnp.zeros((BLOCK, OBS), F32)
    for n in range(BINS):
        factor = jnp.where(distance >= n * LIMIT, taper[0, n].astype(F32), factor)
    effective = weight * (factor / 1024.0)

    has_s, has_n = south.astype(F32), north.astype(F32)
    has_w, has_e = west.astype(F32), east.astype(F32)
    v_pos = (lax.broadcasted_iota(jnp.int32, (TY, K), 0).astype(F32) + 0.5) / TY
    for q, part in enumerate(beta(v_pos, has_s, has_n)):
        by_tab[q] = part

    def beta_x(li):
        return beta(((li & (TX - 1)).astype(F32) + 0.5) / TX, has_w, has_e)

    for k in range(LOADS):
        loads[k].wait()

        def widen(i, _, k=k):
            rows = pl.ds(pl.multiple_of(k * span + i * 256, 256), 256)
            acc[rows, :] = field_v[rows, :].astype(F32)
            return 0

        lax.fori_loop(0, span // 256, widen, 0, unroll=True)

    def pick(i, _):
        for k in range(16):
            s = i * 16 + k
            picked[pl.ds(s, 1), :] = acc[pl.ds(cell_s[0, s], 1), :]
        return 0

    lax.fori_loop(0, OBS // 16, pick, 0)

    mean = jnp.full((K, K), 1.0 / K, BF16)
    cols = lax.broadcasted_iota(jnp.int32, (K, K), 1)
    rows_ = lax.broadcasted_iota(jnp.int32, (K, K), 0)
    eye = (cols == rows_).astype(F32)
    chosen = picked[...]
    chosen_b = chosen.astype(BF16)
    center_b = mm(chosen_b, mean)
    center_r = nt(mean[:16], chosen_b)[:1]
    perturb = (chosen - center_b).astype(BF16)
    perturb_t = nt(eye.astype(BF16), perturb)
    innovation = (value[...] - center_r).astype(BF16).astype(F32)
    spread = jnp.sum(perturb_t * perturb_t, axis=0, keepdims=True) / (K - 1)
    num = weight * innovation * innovation
    den = weight * spread + live
    num = num[:, :K] + num[:, K : 2 * K] + num[:, 2 * K : 3 * K] + num[:, 3 * K :]
    den = den[:, :K] + den[:, K : 2 * K] + den[:, 2 * K : 3 * K] + den[:, 3 * K :]
    num = num + pltpu.roll(num, K // 2, 1)
    den = den + pltpu.roll(den, K // 2, 1)
    lanes = lax.broadcasted_iota(jnp.int32, (1, K), 1)
    sum_a[0] = jnp.where(lanes < K // 2, num, den)

    pl.semaphore_wait(
        barrier,
        BLOCK - 1
        + planes - 1
        + west.astype(jnp.int32)
        + east.astype(jnp.int32)
        + south.astype(jnp.int32)
        + north.astype(jnp.int32),
    )

    def remote(src, dst, send, recv, peer):
        return pltpu.make_async_remote_copy(
            src_ref=src, dst_ref=dst, send_sem=send, recv_sem=recv, device_id=peer, device_id_type=MESH
        )

    ring = [
        remote(sum_a.at[0], sum_a.at[k], send_a.at[k], recv_a.at[k], ring_peer(k))
        for k in range(1, BLOCK)
    ]
    for copy in ring:
        copy.start()

    rhs[:, :K] = perturb
    d_rows = jnp.broadcast_to(innovation, (K, OBS)).T
    rhs[:, K:] = d_rows.astype(BF16)
    for t in range(9):
        weighted[t * K : (t + 1) * K, :] = (perturb_t * effective[t : t + 1, :]).astype(BF16)
    right = rhs[...]
    for t in range(9):
        product = mm(weighted[t * K : (t + 1) * K, :], right)
        gram[t, :K, :] = product[:, :K]
        gram[t, K:, :] = jnp.broadcast_to(
            jnp.sum(product[:, K:] * eye, axis=0, keepdims=True), (GROWS - K, K)
        )

    def for_sides(pairs, act):
        for there, copy in pairs:

            @pl.when(there)
            def _(copy=copy):
                act(copy)

    gx_out = [
        (east, remote(gram.at[pl.ds(0, 3)], gram_x.at[0], send_gx.at[0], recv_gx.at[0], (gx + 1, gy))),
        (west, remote(gram.at[pl.ds(6, 3)], gram_x.at[1], send_gx.at[1], recv_gx.at[1], (gx - 1, gy))),
    ]
    gx_in = [(west, gx_out[0][1]), (east, gx_out[1][1])]
    for_sides(gx_out, lambda copy: copy.start())

    lines = 4

    def prepare(c, _):
        size = lines * TY
        rows = pl.ds(pl.multiple_of(c * size, size), size)
        members = field_v[rows, :]
        center = mm(members, mean)
        acc[rows, :] = center
        deviation = members.astype(F32) - center
        low, middle, top = by_tab[0], by_tab[1], by_tab[2]
        for n in range(lines):
            _, bx, _ = beta_x(c * lines + n)
            piece = deviation[n * TY : (n + 1) * TY]
            at = pl.ds(pl.multiple_of(c * size + n * TY, TY), TY)
            t_ends[at, :K] = (piece * low).astype(BF16)
            t_ends[at, K:] = (piece * top).astype(BF16)
            t_mid[at, :] = (piece * middle).astype(BF16)
            u_side[at, :] = (piece * bx).astype(BF16)
            s_own[at, :] = (piece * (middle * bx)).astype(BF16)
        return 0

    steps = 2 * TX // lines
    lax.fori_loop(0, steps // 2, prepare, 0)

    for copy in ring:
        copy.wait_recv()
    sum_b[0] = jnp.sum(sum_a[...], axis=0)
    cross = [
        remote(sum_b.at[0], sum_b.at[k], send_b.at[k], recv_b.at[k], plane_peer(k))
        for k in range(1, planes)
    ]
    for copy in cross:
        copy.start()

    for_sides(gx_in, lambda copy: copy.wait_recv())
    half[0] = gram[3] + gram_x[0, 0] + gram_x[1, 0]
    half[1] = gram[5] + gram_x[0, 2] + gram_x[1, 2]
    gy_out = [
        (north, remote(half.at[0], gram_y.at[0], send_gy.at[0], recv_gy.at[0], (gx, gy + 1))),
        (south, remote(half.at[1], gram_y.at[1], send_gy.at[1], recv_gy.at[1], (gx, gy - 1))),
    ]
    gy_in = [(south, gy_out[0][1]), (north, gy_out[1][1])]
    for_sides(gy_out, lambda copy: copy.start())

    lax.fori_loop(steps // 2, steps, prepare, 0)

    for_sides(gy_in, lambda copy: copy.wait_recv())
    total = gram[4] + gram_x[0, 1] + gram_x[1, 1] + gram_y[0] + gram_y[1]
    projected = jnp.broadcast_to(total[K : K + 1], (K, K)).T
    total = total[:K]

    for copy in cross:
        copy.wait_recv()
    sums = jnp.sum(sum_b[...], axis=0)
    numerator = jnp.sum(jnp.where(lanes < K // 2, sums, 0.0), axis=1, keepdims=True)
    denominator = jnp.sum(jnp.where(lanes < K // 2, 0.0, sums), axis=1, keepdims=True)
    inflation = numerator / denominator

    system = eye / inflation + total / (K - 1)
    frob = jnp.sqrt(jnp.sum(jnp.sum(system * system, axis=0, keepdims=True), axis=1, keepdims=True))
    root = system / frob
    inv_root = None
    for sweep in range(NSTEPS):
        joint = root if sweep == 0 else high(inv_root, root)
        correction = 1.5 * eye - 0.5 * joint
        if sweep < NSTEPS - 1:
            root = high(root, correction)
        inv_root = correction if sweep == 0 else high(correction, inv_root)
    shift = high(inv_root, high(inv_root, projected)) / (frob * (K - 1))
    w_all[1, 1] = (inv_root / jnp.sqrt(frob) + shift).astype(BF16)

    mine = w_all.at[1, 1]
    wy_out = [
        (north, remote(mine, w_all.at[1, 0], send_wy.at[0], recv_wy.at[0], (gx, gy + 1))),
        (south, remote(mine, w_all.at[1, 2], send_wy.at[1], recv_wy.at[1], (gx, gy - 1))),
    ]
    wy_in = [(south, wy_out[0][1]), (north, wy_out[1][1])]
    wx_out = [
        (east, remote(mine, w_all.at[0, 1], send_wx.at[0], recv_wx.at[0], (gx + 1, gy))),
        (west, remote(mine, w_all.at[2, 1], send_wx.at[1], recv_wx.at[1], (gx - 1, gy))),
    ]
    wx_in = [(west, wx_out[0][1]), (east, wx_out[1][1])]
    for_sides(wy_out, lambda copy: copy.start())
    for_sides(wx_out, lambda copy: copy.start())

    wide = 8
    size = wide * TY

    def own(c, _):
        rows = pl.ds(pl.multiple_of(c * size, size), size)
        acc[rows, :] = acc[rows, :] + mm(s_own[rows, :], w_all[1, 1])
        return 0

    lax.fori_loop(0, CELLS // size, own, 0)

    for_sides(wy_in, lambda copy: copy.wait_recv())
    wc_out = []
    wc_in = []
    for n, (from_y, q) in enumerate(((south, 0), (north, 2))):
        to_e = remote(w_all.at[1, q], w_all.at[0, q], send_wc.at[0, n], recv_wc.at[0, n], (gx + 1, gy))
        to_w = remote(w_all.at[1, q], w_all.at[2, q], send_wc.at[1, n], recv_wc.at[1, n], (gx - 1, gy))
        wc_out += [(jnp.logical_and(from_y, east), to_e), (jnp.logical_and(from_y, west), to_w)]
        wc_in += [(jnp.logical_and(from_y, west), to_e), (jnp.logical_and(from_y, east), to_w)]
    for_sides(wc_out, lambda copy: copy.start())
    for_sides(wx_in, lambda copy: copy.wait_recv())

    def edges(c, _):
        rows = pl.ds(pl.multiple_of(c * size, size), size)
        along_x = mm(t_mid[rows, :], jnp.concatenate([w_all[0, 1], w_all[2, 1]], axis=1))
        along_y = mm(u_side[rows, :], jnp.concatenate([w_all[1, 0], w_all[1, 2]], axis=1))
        for n in range(wide):
            bl, _, bh = beta_x(c * wide + n)
            cut = slice(n * TY, (n + 1) * TY)
            at = pl.ds(pl.multiple_of(c * size + n * TY, TY), TY)
            acc[at, :] = (
                acc[at, :]
                + (bl * along_x[cut, :K] + bh * along_x[cut, K:])
                + (by_tab[0] * along_y[cut, :K] + by_tab[2] * along_y[cut, K:])
            )
        return 0

    lax.fori_loop(0, CELLS // size, edges, 0)

    for_sides(wc_in, lambda copy: copy.wait_recv())

    def corners(c, _):
        rows = pl.ds(pl.multiple_of(c * size, size), size)
        ends = jnp.concatenate(
            [
                jnp.concatenate([w_all[0, 0], w_all[2, 0]], axis=1),
                jnp.concatenate([w_all[0, 2], w_all[2, 2]], axis=1),
            ],
            axis=0,
        )
        product = mm(t_ends[rows, :], ends)
        for n in range(wide):
            bl, _, bh = beta_x(c * wide + n)
            cut = slice(n * TY, (n + 1) * TY)
            at = pl.ds(pl.multiple_of(c * size + n * TY, TY), TY)
            out[at, :] = (acc[at, :] + (bl * product[cut, :K] + bh * product[cut, K:])).astype(BF16)
        return 0

    lax.fori_loop(0, CELLS // size, corners, 0)

    for copy in ring + cross:
        copy.wait_send()
    for_sides(gx_out + gy_out + wy_out + wx_out + wc_out, lambda copy: copy.wait_send())


def local(n_gx, n_gy, background, cell_index, obs_value, obs_inverse, obs_count, taper):
    levels, tile_x, tile_y, members = background.shape
    field = background.reshape(-1, members)
    cells = cell_index.reshape(1, OBS)
    smem = pl.BlockSpec(memory_space=pltpu.SMEM)
    vmem = pl.BlockSpec(memory_space=pltpu.VMEM)
    dma = pltpu.SemaphoreType.DMA
    planes = n_gx // BLOCK * n_gy
    result = pl.pallas_call(
        functools.partial(kernel, n_gx, n_gy),
        out_shape=jax.ShapeDtypeStruct((CELLS, K), BF16),
        in_specs=[pl.BlockSpec(memory_space=pltpu.HBM), smem, vmem, vmem, vmem, smem, smem],
        out_specs=vmem,
        scratch_shapes=[
            pltpu.VMEM((CELLS, K), BF16),
            pltpu.VMEM((CELLS, K), F32),
            pltpu.VMEM((CELLS, K), BF16),
            pltpu.VMEM((CELLS, K), BF16),
            pltpu.VMEM((CELLS, K), BF16),
            pltpu.VMEM((CELLS, 2 * K), BF16),
            pltpu.VMEM((3, TY, K), F32),
            pltpu.VMEM((OBS, K), F32),
            pltpu.VMEM((9 * K, OBS), BF16),
            pltpu.VMEM((OBS, 2 * K), BF16),
            pltpu.VMEM((9, GROWS, K), F32),
            pltpu.VMEM((2, 3, GROWS, K), F32),
            pltpu.VMEM((2, GROWS, K), F32),
            pltpu.VMEM((2, GROWS, K), F32),
            pltpu.VMEM((BLOCK, 1, K), F32),
            pltpu.VMEM((planes, 1, K), F32),
            pltpu.VMEM((3, 3, K, K), BF16),
            dma((LOADS,)),
            dma((BLOCK,)),
            dma((BLOCK,)),
            dma((planes,)),
            dma((planes,)),
            dma((2,)),
            dma((2,)),
            dma((2,)),
            dma((2,)),
            dma((2,)),
            dma((2,)),
            dma((2,)),
            dma((2,)),
            dma((2, 2)),
            dma((2, 2)),
        ],
        compiler_params=pltpu.CompilerParams(
            collective_id=0, has_side_effects=True, vmem_limit_bytes=60 * 1024 * 1024
        ),
    )(
        field,
        cells,
        cells,
        obs_value.reshape(1, OBS),
        obs_inverse.reshape(1, OBS),
        obs_count.reshape(1, 1),
        taper.reshape(1, BINS),
    )
    return result.reshape(levels, tile_x, tile_y, members)


def solution(mesh):
    in_specs = (
        P(None, "gx", "gy", None),
        P("gx", "gy", None),
        P("gx", "gy", None),
        P("gx", "gy", None),
        P("gx", "gy"),
        P(),
    )
    out_specs = P(None, "gx", "gy", None)
    step = functools.partial(local, mesh.shape["gx"], mesh.shape["gy"])
    return jax.shard_map(step, mesh=mesh, in_specs=in_specs, out_specs=out_specs, check_vma=False)
```

time: 186 us -> 48.1 us (0.26); the launches traced: 184 us -> 48 us
  blocking collectives: 77.6 us -> 0 us
  Pallas kernels: 0 us -> 42.5 us
  matrix products: 30.8 us -> 0 us
  starting transfers between devices: 28.5 us -> 0 us
  other arithmetic: 27.2 us -> 0 us
  waiting for transfers between devices: 11.6 us -> 0 us
  between operations: 4.26 us -> 0.66 us
    psum x1 -> x0, blocking collectives: 77.6 us -> none  [local(): numerator, denominator = lax.psum((numerator, denominator), ('gx', 'gy'))]
    pallas_call x0 -> x1, Pallas kernels: none -> 42.5 us  [local(): pl.pallas_call(functools.partial(kernel, n_gx, n_gy), out_shape=jax.Shape...]
    dot_general x24 -> x0, matrix products: 30.8 us -> none  [the longest x3 25.6 us: blend(): product = jnp.dot(stacked, column_stack, preferred_element_type=jnp.float32)]
    ppermute x8 -> x0, starting transfers between devices: 28.5 us -> none  [the longest x4 19.7 us: extended(): lax.ppermute(head, axis, [((i + 1) % count, i) for i in range(ends)])]
    convert_element_type x6 -> x0, other arithmetic: 18.9 us -> none  [the longest x1 17.4 us: blend(): pieces = [(deviation * (beta_x[offset_x][:, None] * beta_y[offset_y][None...]
    ppermute x8 -> x0, waiting for transfers between devices: 11.6 us -> none  [the longest x4 7.03 us: extended(): lax.ppermute(head, axis, [((i + 1) % count, i) for i in range(ends)])]
    reduce_sum x6 -> x0, other arithmetic: 5.49 us -> none  [the longest x1 3.36 us: blend(): center = jnp.mean(widened, axis=-1, keepdims=True)]
    unnamed x2 -> x1, local copies, waits for them, and re-layouts: 0.01 us -> 4.79 us
  transfers between devices with their start and end apart: 8 -> 0, of which waited for: 2 -> 0; matrix products, arithmetic and copies ran while one was open for 20% -> 0% of each run, Pallas kernels for 0% -> 0%
where the time goes in v1:
time: 48.1 us; the launch traced here: 48 us
  Pallas kernels  42.5 us (88%)
  local copies, waits for them, and re-layouts  4.79 us (10%)
  between operations  0.66 us (1%)
    pallas_call x1, Pallas kernels, local(): pl.pallas_call(functools.partial(kernel, n_gx, n_gy), out_shape=jax.Shape...  42.5 us
    unnamed x1, local copies, waits for them, and re-layouts  4.79 us

profile of v1, /device:TPU:6, one launch (start us, length us, event | category | flops | bytes accessed | tf_op | source)
XLA Modules:
  0.0 48.0 jit_solution(12938968162864636885)
XLA Ops:
  0.7 42.5 %shard_map.64 = bf16[16384,128]{1,0:T(8,128)(2,1)} custom-call(bf16[16384,128]{1,0:T(8,128)(2,1)} %bitcast.7, s32[1,512]{1,0:T(1,128)} %bitcast.8, s32[1,512]{1,0:T(1,128)} %bitcast.9, f32[1,512]{1,0:T(1,128)} %bitcast.10, f32[1,512]{1,0:T(1,128)} %bitcast.11, s32[1,1]{1,0:T(1,128)S(6)} %copy.8.count, s32[1,64]{1,0:T(1,128)} %bitcast.12), custom_call_target="tpu_custom_call" | custom-call | tf_op jit(solution)/shard_map/pallas_call | solution.py:410
  43.2 4.8 %copy.9 = bf16[2,64,128,128]{3,2,1,0:T(8,128)(2,1)} copy(bf16[2,64,128,128]{3,2,1,0:T(8,128)(2,1)} %bitcast.6) | data formatting | bytes 8388608

commit v2 on v1

--- a/solution.py
+++ b/solution.py
@@ -45,6 +45,35 @@
     return low * has_low, middle, top * has_high
 
 
+def by_line(table, p, line, x):
+    return (x.reshape(TY // 8, 8, K) * table[p, line][None]).reshape(TY, K)
+
+
+def last_pass(acc, scaled, sides_w, bx_tab, out, result, out_sem):
+    size = 16 * TY
+    copies = [
+        pltpu.make_async_copy(
+            result.at[pl.ds(c * size, size), :], out.at[pl.ds(c * size, size), :], out_sem.at[c]
+        )
+        for c in range(CELLS // size)
+    ]
+
+    for c in range(CELLS // size):
+        product = mm(scaled[c * size : (c + 1) * size, :], sides_w[...])
+        for n in range(size // TY):
+            line = (c * (size // TY) + n) % TX
+            cut = slice(n * TY, (n + 1) * TY)
+            at = slice(c * size + n * TY, c * size + (n + 1) * TY)
+            result[at, :] = (
+                acc[at, :]
+                + by_line(bx_tab, 0, line, product[cut, :K])
+                + by_line(bx_tab, 2, line, product[cut, K:])
+            ).astype(BF16)
+        copies[c].start()
+    for copy in copies:
+        copy.wait()
+
+
 def kernel(
     n_gx,
     n_gy,
@@ -55,13 +84,13 @@
     inverse,
     count,
     taper,
-    out,
+    acc,
+    scaled,
+    sides_w,
+    bx_tab,
     field_v,
-    acc,
     s_own,
     u_side,
-    t_mid,
-    t_ends,
     by_tab,
     picked,
     weighted,
@@ -159,8 +188,9 @@
     for q, part in enumerate(beta(v_pos, has_s, has_n)):
         by_tab[q] = part
 
-    def beta_x(li):
-        return beta(((li & (TX - 1)).astype(F32) + 0.5) / TX, has_w, has_e)
+    u_pos = (lax.broadcasted_iota(jnp.int32, (TX, 8, K), 0).astype(F32) + 0.5) / TX
+    for p, part in enumerate(beta(u_pos, has_w, has_e)):
+        bx_tab[p] = part
 
     for k in range(LOADS):
         loads[k].wait()
@@ -250,7 +280,7 @@
     gx_in = [(west, gx_out[0][1]), (east, gx_out[1][1])]
     for_sides(gx_out, lambda copy: copy.start())
 
-    lines = 4
+    lines = 8
 
     def prepare(c, _):
         size = lines * TY
@@ -261,14 +291,14 @@
         deviation = members.astype(F32) - center
         low, middle, top = by_tab[0], by_tab[1], by_tab[2]
         for n in range(lines):
-            _, bx, _ = beta_x(c * lines + n)
+            line = (c * lines + n) & (TX - 1)
             piece = deviation[n * TY : (n + 1) * TY]
             at = pl.ds(pl.multiple_of(c * size + n * TY, TY), TY)
-            t_ends[at, :K] = (piece * low).astype(BF16)
-            t_ends[at, K:] = (piece * top).astype(BF16)
-            t_mid[at, :] = (piece * middle).astype(BF16)
-            u_side[at, :] = (piece * bx).astype(BF16)
-            s_own[at, :] = (piece * (middle * bx)).astype(BF16)
+            scaled[at, :K] = (piece * low).astype(BF16)
+            scaled[at, K : 2 * K] = (piece * middle).astype(BF16)
+            scaled[at, 2 * K :] = (piece * top).astype(BF16)
+            u_side[at, :] = by_line(bx_tab, 1, line, piece).astype(BF16)
+            s_own[at, :] = (piece * by_line(bx_tab, 1, line, middle)).astype(BF16)
         return 0
 
     steps = 2 * TX // lines
@@ -335,15 +365,14 @@
     for_sides(wy_out, lambda copy: copy.start())
     for_sides(wx_out, lambda copy: copy.start())
 
-    wide = 8
-    size = wide * TY
+    size = 16 * TY
 
     def own(c, _):
         rows = pl.ds(pl.multiple_of(c * size, size), size)
         acc[rows, :] = acc[rows, :] + mm(s_own[rows, :], w_all[1, 1])
         return 0
 
-    lax.fori_loop(0, CELLS // size, own, 0)
+    lax.fori_loop(0, CELLS // size, own, 0, unroll=2)
 
     for_sides(wy_in, lambda copy: copy.wait_recv())
     wc_out = []
@@ -354,45 +383,24 @@
         wc_out += [(jnp.logical_and(from_y, east), to_e), (jnp.logical_and(from_y, west), to_w)]
         wc_in += [(jnp.logical_and(from_y, west), to_e), (jnp.logical_and(from_y, east), to_w)]
     for_sides(wc_out, lambda copy: copy.start())
-    for_sides(wx_in, lambda copy: copy.wait_recv())
-
-    def edges(c, _):
+
+    def along_gy(c, _):
         rows = pl.ds(pl.multiple_of(c * size, size), size)
-        along_x = mm(t_mid[rows, :], jnp.concatenate([w_all[0, 1], w_all[2, 1]], axis=1))
-        along_y = mm(u_side[rows, :], jnp.concatenate([w_all[1, 0], w_all[1, 2]], axis=1))
-        for n in range(wide):
-            bl, _, bh = beta_x(c * wide + n)
+        product = mm(u_side[rows, :], jnp.concatenate([w_all[1, 0], w_all[1, 2]], axis=1))
+        low, top = by_tab[0], by_tab[2]
+        for n in range(size // TY):
             cut = slice(n * TY, (n + 1) * TY)
             at = pl.ds(pl.multiple_of(c * size + n * TY, TY), TY)
-            acc[at, :] = (
-                acc[at, :]
-                + (bl * along_x[cut, :K] + bh * along_x[cut, K:])
-                + (by_tab[0] * along_y[cut, :K] + by_tab[2] * along_y[cut, K:])
-            )
+            acc[at, :] = acc[at, :] + (low * product[cut, :K] + top * product[cut, K:])
         return 0
 
-    lax.fori_loop(0, CELLS // size, edges, 0)
-
+    lax.fori_loop(0, CELLS // size, along_gy, 0, unroll=2)
+
+    for_sides(wx_in, lambda copy: copy.wait_recv())
     for_sides(wc_in, lambda copy: copy.wait_recv())
-
-    def corners(c, _):
-        rows = pl.ds(pl.multiple_of(c * size, size), size)
-        ends = jnp.concatenate(
-            [
-                jnp.concatenate([w_all[0, 0], w_all[2, 0]], axis=1),
-                jnp.concatenate([w_all[0, 2], w_all[2, 2]], axis=1),
-            ],
-            axis=0,
-        )
-        product = mm(t_ends[rows, :], ends)
-        for n in range(wide):
-            bl, _, bh = beta_x(c * wide + n)
-            cut = slice(n * TY, (n + 1) * TY)
-            at = pl.ds(pl.multiple_of(c * size + n * TY, TY), TY)
-            out[at, :] = (acc[at, :] + (bl * product[cut, :K] + bh * product[cut, K:])).astype(BF16)
-        return 0
-
-    lax.fori_loop(0, CELLS // size, corners, 0)
+    for q in range(3):
+        sides_w[q * K : (q + 1) * K, :K] = w_all[0, q]
+        sides_w[q * K : (q + 1) * K, K:] = w_all[2, q]
 
     for copy in ring + cross:
         copy.wait_send()
@@ -407,18 +415,20 @@
     vmem = pl.BlockSpec(memory_space=pltpu.VMEM)
     dma = pltpu.SemaphoreType.DMA
     planes = n_gx // BLOCK * n_gy
-    result = pl.pallas_call(
+    parts = pl.pallas_call(
         functools.partial(kernel, n_gx, n_gy),
-        out_shape=jax.ShapeDtypeStruct((CELLS, K), BF16),
+        out_shape=(
+            pltpu.VMEM((CELLS, K), F32),
+            pltpu.VMEM((CELLS, 3 * K), BF16),
+            pltpu.VMEM((3 * K, 2 * K), BF16),
+            pltpu.VMEM((3, TX, 8, K), F32),
+        ),
         in_specs=[pl.BlockSpec(memory_space=pltpu.HBM), smem, vmem, vmem, vmem, smem, smem],
-        out_specs=vmem,
+        out_specs=(vmem, vmem, vmem, vmem),
         scratch_shapes=[
-            pltpu.VMEM((CELLS, K), BF16),
-            pltpu.VMEM((CELLS, K), F32),
             pltpu.VMEM((CELLS, K), BF16),
             pltpu.VMEM((CELLS, K), BF16),
             pltpu.VMEM((CELLS, K), BF16),
-            pltpu.VMEM((CELLS, 2 * K), BF16),
             pltpu.VMEM((3, TY, K), F32),
             pltpu.VMEM((OBS, K), F32),
             pltpu.VMEM((9 * K, OBS), BF16),
@@ -447,7 +457,7 @@
             dma((2, 2)),
         ],
         compiler_params=pltpu.CompilerParams(
-            collective_id=0, has_side_effects=True, vmem_limit_bytes=60 * 1024 * 1024
+            collective_id=0, has_side_effects=True, vmem_limit_bytes=20 * 1024 * 1024
         ),
     )(
         field,
@@ -458,6 +468,14 @@
         obs_count.reshape(1, 1),
         taper.reshape(1, BINS),
     )
+    result = pl.pallas_call(
+        last_pass,
+        out_shape=jax.ShapeDtypeStruct((CELLS, K), BF16),
+        in_specs=[vmem] * 4,
+        out_specs=pl.BlockSpec(memory_space=pltpu.HBM),
+        scratch_shapes=[pltpu.VMEM((CELLS, K), BF16), dma((CELLS // (16 * TY),))],
+        compiler_params=pltpu.CompilerParams(vmem_limit_bytes=16 * 1024 * 1024),
+    )(*parts)
     return result.reshape(levels, tile_x, tile_y, members)
 
 

time: 48.1 us -> 43.7 us (0.909)
  Pallas kernels: 42.5 us -> 37.9 us
    pallas_call x1 -> x2, Pallas kernels: 42.5 us -> 37.9 us  [the longest x1 32.2 us: local(): pl.pallas_call(functools.partial(kernel, n_gx, n_gy), out_shape=(pltpu.VM...]
    unnamed x1 -> x10, local copies, waits for them, and re-layouts: 4.79 us -> 4.88 us
where the time goes in v2:
time: 43.7 us; the launch traced here: 43.5 us
  Pallas kernels  37.9 us (87%)
  local copies, waits for them, and re-layouts  4.88 us (11%)
  between operations  0.67 us (2%)
    pallas_call x1, Pallas kernels, local(): pl.pallas_call(functools.partial(kernel, n_gx, n_gy), out_shape=(pltpu.VM...  32.2 us
    pallas_call x1, Pallas kernels, local(): pl.pallas_call(last_pass, out_shape=jax.ShapeDtypeStruct((CELLS, K), BF16...  5.74 us
    unnamed x10, local copies, waits for them, and re-layouts  4.88 us

profile of v2, /device:TPU:6, one launch (start us, length us, event | category | flops | bytes accessed | tf_op | source)
XLA Modules:
  0.0 43.5 jit_solution(12488552617431511011)
XLA Ops:
  0.7 0.0 copy-start
  0.7 2.2 %copy-done = bf16[2,64,128,128]{3,2,1,0:T(8,128)(2,1)S(1)} copy-done((bf16[2,64,128,128]{3,2,1,0:T(8,128)(2,1)S(1)}, bf16[2,64,128,128]{3,2,1,0:T(8,128)(2,1)}, u32[]{:S(2)}) %copy-start) | copy-done | bytes 4194328
  2.8 0.0 copy-start.1
  2.8 0.7 %copy-done.1 = s32[1,1,512]{2,1,0:T(1,128)S(1)} copy-done((s32[1,1,512]{2,1,0:T(1,128)S(1)}, s32[1,1,512]{2,1,0:T(1,128)}, u32[]{:S(2)}) %copy-start.1) | copy-done | bytes 2072
  3.5 0.0 copy-start.2
  3.5 0.7 %copy-done.2 = f32[1,1,512]{2,1,0:T(1,128)S(1)} copy-done((f32[1,1,512]{2,1,0:T(1,128)S(1)}, f32[1,1,512]{2,1,0:T(1,128)}, u32[]{:S(2)}) %copy-start.2) | copy-done | bytes 2072
  4.2 0.0 copy-start.3
  4.2 0.7 %copy-done.3 = f32[1,1,512]{2,1,0:T(1,128)S(1)} copy-done((f32[1,1,512]{2,1,0:T(1,128)S(1)}, f32[1,1,512]{2,1,0:T(1,128)}, u32[]{:S(2)}) %copy-start.3) | copy-done | bytes 2072
  4.9 0.0 copy-start.4
  4.9 0.7 %copy-done.4 = s32[64]{0:T(128)S(1)} copy-done((s32[64]{0:T(128)S(1)}, s32[64]{0:T(128)}, u32[]{:S(2)}) %copy-start.4) | copy-done | bytes 280
  5.5 32.2 %shard_map.64 = (f32[16384,128]{1,0:T(8,128)S(1)}, bf16[16384,384]{1,0:T(8,128)(2,1)S(1)}, bf16[384,256]{1,0:T(8,128)(2,1)S(1)}, f32[3,64,8,128]{3,2,1,0:T(8,128)S(1)}) custom-call(bf16[16384,128]{1,0:T(8,128)(2,1)S(1)} %bitcast.6, s32[1,512]{1,0:T(1,128)S(1)} %bitcast.7, s32[1,512]{1,0:T(1,128)S(1)} %bitcast.8, f32[1,512]{1,0:T(1,128)S(1)} %bitcast.9, ...), custom_call_target="tpu_custom_call" | custom-call | tf_op jit(solution)/shard_map/pallas_call | solution.py:418
  37.7 5.7 %shard_map.65 = bf16[16384,128]{1,0:T(8,128)(2,1)} custom-call(f32[16384,128]{1,0:T(8,128)S(1)} %get-tuple-element.9.acc, bf16[16384,384]{1,0:T(8,128)(2,1)S(1)} %get-tuple-element.10.scaled, bf16[384,256]{1,0:T(8,128)(2,1)S(1)} %get-tuple-element.11.sides_w, f32[3,64,8,128]{3,2,1,0:T(8,128)S(1)} %get-tuple-element.12.bx_tab), custom_call_target="tpu_custom_call" | custom-call | tf_op jit(solution)/shard_map/pallas_call | solution.py:471
Async XLA Ops:
  0.7 2.2 %copy-start = (bf16[2,64,128,128]{3,2,1,0:T(8,128)(2,1)S(1)}, bf16[2,64,128,128]{3,2,1,0:T(8,128)(2,1)}, u32[]{:S(2)}) copy-start(bf16[2,64,128,128]{3,2,1,0:T(8,128)(2,1)} %param.6) | copy-start | bytes 12582916
  2.8 0.7 %copy-start.1 = (s32[1,1,512]{2,1,0:T(1,128)S(1)}, s32[1,1,512]{2,1,0:T(1,128)}, u32[]{:S(2)}) copy-start(s32[1,1,512]{2,1,0:T(1,128)} %param.7) | copy-start | bytes 6148
  3.5 0.7 %copy-start.2 = (f32[1,1,512]{2,1,0:T(1,128)S(1)}, f32[1,1,512]{2,1,0:T(1,128)}, u32[]{:S(2)}) copy-start(f32[1,1,512]{2,1,0:T(1,128)} %param.8) | copy-start | bytes 6148
  4.2 0.7 %copy-start.3 = (f32[1,1,512]{2,1,0:T(1,128)S(1)}, f32[1,1,512]{2,1,0:T(1,128)}, u32[]{:S(2)}) copy-start(f32[1,1,512]{2,1,0:T(1,128)} %param.9) | copy-start | bytes 6148
  4.9 0.7 %copy-start.4 = (s32[64]{0:T(128)S(1)}, s32[64]{0:T(128)}, u32[]{:S(2)}) copy-start(s32[64]{0:T(128)} %param.11) | copy-start | bytes 772

commit v3 on v2

--- a/solution.py
+++ b/solution.py
@@ -8,7 +8,6 @@
 from jax.sharding import PartitionSpec as P
 
 NSTEPS = 6
-HIGH = lax.Precision.HIGHEST
 MESH = pl.DeviceIdType.MESH
 F32 = jnp.float32
 BF16 = jnp.bfloat16
@@ -33,8 +32,14 @@
     return jnp.dot(a, b, preferred_element_type=F32)
 
 
-def high(a, b):
-    return jnp.dot(a, b, precision=HIGH, preferred_element_type=F32)
+def product3(a, b):
+    a_top, b_top = a.astype(BF16), b.astype(BF16)
+    a_rest = (a - a_top.astype(F32)).astype(BF16)
+    b_rest = (b - b_top.astype(F32)).astype(BF16)
+    return mm(
+        jnp.concatenate([a_top, a_rest, a_top], axis=1),
+        jnp.concatenate([b_top, b_top, b_rest], axis=0),
+    )
 
 
 def beta(position, has_low, has_high):
@@ -78,12 +83,11 @@
     n_gx,
     n_gy,
     field,
-    cell_s,
-    cell_v,
-    value,
-    inverse,
+    cell_h,
+    value_h,
+    inverse_h,
     count,
-    taper,
+    taper_h,
     acc,
     scaled,
     sides_w,
@@ -92,6 +96,11 @@
     s_own,
     u_side,
     by_tab,
+    cell_s,
+    cell_v,
+    value,
+    inverse,
+    taper,
     picked,
     weighted,
     rhs,
@@ -103,6 +112,7 @@
     sum_b,
     w_all,
     load_sem,
+    small_sem,
     send_a,
     recv_a,
     send_b,
@@ -127,8 +137,20 @@
         )
         for k in range(LOADS)
     ]
-    for load in loads:
-        load.start()
+    small = [
+        pltpu.make_async_copy(source, target, small_sem.at[k])
+        for k, (source, target) in enumerate(
+            (
+                (cell_h, cell_v),
+                (taper_h, taper),
+                (inverse_h, inverse),
+                (value_h, value),
+                (cell_h, cell_s),
+            )
+        )
+    ]
+    for copy in small + loads:
+        copy.start()
 
     gram_x[...] = jnp.zeros_like(gram_x)
     gram_y[...] = jnp.zeros_like(gram_y)
@@ -165,6 +187,19 @@
         @pl.when(there)
         def _(peer=peer):
             pl.semaphore_signal(barrier, inc=1, device_id=peer, device_id_type=MESH)
+
+    has_s, has_n = south.astype(F32), north.astype(F32)
+    has_w, has_e = west.astype(F32), east.astype(F32)
+    v_pos = (lax.broadcasted_iota(jnp.int32, (TY, K), 0).astype(F32) + 0.5) / TY
+    for q, part in enumerate(beta(v_pos, has_s, has_n)):
+        by_tab[q] = part
+
+    u_pos = (lax.broadcasted_iota(jnp.int32, (TX, 8, K), 0).astype(F32) + 0.5) / TX
+    for p, part in enumerate(beta(u_pos, has_w, has_e)):
+        bx_tab[p] = part
+
+    for copy in small:
+        copy.wait()
 
     cells = cell_v[...]
     col = lax.shift_right_logical(cells & (TX * TY - 1), 7)
@@ -181,16 +216,6 @@
     for n in range(BINS):
         factor = jnp.where(distance >= n * LIMIT, taper[0, n].astype(F32), factor)
     effective = weight * (factor / 1024.0)
-
-    has_s, has_n = south.astype(F32), north.astype(F32)
-    has_w, has_e = west.astype(F32), east.astype(F32)
-    v_pos = (lax.broadcasted_iota(jnp.int32, (TY, K), 0).astype(F32) + 0.5) / TY
-    for q, part in enumerate(beta(v_pos, has_s, has_n)):
-        by_tab[q] = part
-
-    u_pos = (lax.broadcasted_iota(jnp.int32, (TX, 8, K), 0).astype(F32) + 0.5) / TX
-    for p, part in enumerate(beta(u_pos, has_w, has_e)):
-        bx_tab[p] = part
 
     for k in range(LOADS):
         loads[k].wait()
@@ -302,7 +327,7 @@
         return 0
 
     steps = 2 * TX // lines
-    lax.fori_loop(0, steps // 2, prepare, 0)
+    lax.fori_loop(0, steps // 2, prepare, 0, unroll=2)
 
     for copy in ring:
         copy.wait_recv()
@@ -324,7 +349,7 @@
     gy_in = [(south, gy_out[0][1]), (north, gy_out[1][1])]
     for_sides(gy_out, lambda copy: copy.start())
 
-    lax.fori_loop(steps // 2, steps, prepare, 0)
+    lax.fori_loop(steps // 2, steps, prepare, 0, unroll=2)
 
     for_sides(gy_in, lambda copy: copy.wait_recv())
     total = gram[4] + gram_x[0, 1] + gram_x[1, 1] + gram_y[0] + gram_y[1]
@@ -341,14 +366,18 @@
     system = eye / inflation + total / (K - 1)
     frob = jnp.sqrt(jnp.sum(jnp.sum(system * system, axis=0, keepdims=True), axis=1, keepdims=True))
     root = system / frob
-    inv_root = None
-    for sweep in range(NSTEPS):
-        joint = root if sweep == 0 else high(inv_root, root)
-        correction = 1.5 * eye - 0.5 * joint
-        if sweep < NSTEPS - 1:
-            root = high(root, correction)
-        inv_root = correction if sweep == 0 else high(correction, inv_root)
-    shift = high(inv_root, high(inv_root, projected)) / (frob * (K - 1))
+    correction = 1.5 * eye - 0.5 * root
+    root = product3(correction, root)
+    inv_root = correction
+    for sweep in range(1, NSTEPS - 1):
+        correction = 1.5 * eye - 0.5 * product3(inv_root, root)
+        both = product3(correction, jnp.concatenate([root, inv_root], axis=1))
+        root, inv_root = both[:, :K], both[:, K:]
+    both = product3(inv_root, jnp.concatenate([root, projected], axis=1))
+    correction = 1.5 * eye - 0.5 * both[:, :K]
+    both = product3(correction, jnp.concatenate([inv_root, both[:, K:]], axis=1))
+    inv_root = both[:, :K]
+    shift = product3(inv_root, both[:, K:]) / (frob * (K - 1))
     w_all[1, 1] = (inv_root / jnp.sqrt(frob) + shift).astype(BF16)
 
     mine = w_all.at[1, 1]
@@ -411,10 +440,11 @@
     levels, tile_x, tile_y, members = background.shape
     field = background.reshape(-1, members)
     cells = cell_index.reshape(1, OBS)
-    smem = pl.BlockSpec(memory_space=pltpu.SMEM)
     vmem = pl.BlockSpec(memory_space=pltpu.VMEM)
+    hbm = pl.BlockSpec(memory_space=pltpu.HBM)
     dma = pltpu.SemaphoreType.DMA
     planes = n_gx // BLOCK * n_gy
+    pin = functools.partial(pltpu.with_memory_space_constraint, memory_space=pltpu.HBM)
     parts = pl.pallas_call(
         functools.partial(kernel, n_gx, n_gy),
         out_shape=(
@@ -423,13 +453,18 @@
             pltpu.VMEM((3 * K, 2 * K), BF16),
             pltpu.VMEM((3, TX, 8, K), F32),
         ),
-        in_specs=[pl.BlockSpec(memory_space=pltpu.HBM), smem, vmem, vmem, vmem, smem, smem],
+        in_specs=[hbm, hbm, hbm, hbm, pl.BlockSpec(memory_space=pltpu.SMEM), hbm],
         out_specs=(vmem, vmem, vmem, vmem),
         scratch_shapes=[
             pltpu.VMEM((CELLS, K), BF16),
             pltpu.VMEM((CELLS, K), BF16),
             pltpu.VMEM((CELLS, K), BF16),
             pltpu.VMEM((3, TY, K), F32),
+            pltpu.SMEM((1, OBS), jnp.int32),
+            pltpu.VMEM((1, OBS), jnp.int32),
+            pltpu.VMEM((1, OBS), F32),
+            pltpu.VMEM((1, OBS), F32),
+            pltpu.SMEM((1, BINS), jnp.int32),
             pltpu.VMEM((OBS, K), F32),
             pltpu.VMEM((9 * K, OBS), BF16),
             pltpu.VMEM((OBS, 2 * K), BF16),
@@ -441,6 +476,7 @@
             pltpu.VMEM((planes, 1, K), F32),
             pltpu.VMEM((3, 3, K, K), BF16),
             dma((LOADS,)),
+            dma((5,)),
             dma((BLOCK,)),
             dma((BLOCK,)),
             dma((planes,)),
@@ -460,13 +496,12 @@
             collective_id=0, has_side_effects=True, vmem_limit_bytes=20 * 1024 * 1024
         ),
     )(
-        field,
-        cells,
-        cells,
-        obs_value.reshape(1, OBS),
-        obs_inverse.reshape(1, OBS),
+        pin(field),
+        pin(cells),
+        pin(obs_value.reshape(1, OBS)),
+        pin(obs_inverse.reshape(1, OBS)),
         obs_count.reshape(1, 1),
-        taper.reshape(1, BINS),
+        pin(taper.reshape(1, BINS)),
     )
     result = pl.pallas_call(
         last_pass,

time: 43.7 us -> 36.7 us (0.84)
  local copies, waits for them, and re-layouts: 4.88 us -> 0 us
  Pallas kernels: 37.9 us -> 36 us
    unnamed x10 -> x0, local copies, waits for them, and re-layouts: 4.88 us -> none
    pallas_call x1, Pallas kernels: 32.2 us -> 30.2 us  [local(): pl.pallas_call(functools.partial(kernel, n_gx, n_gy), out_shape=(pltpu.VM...]
where the time goes in v3:
time: 36.7 us; the launch traced here: 36.6 us
  Pallas kernels  36 us (98%)
  between operations  0.66 us (2%)
    pallas_call x1, Pallas kernels, local(): pl.pallas_call(functools.partial(kernel, n_gx, n_gy), out_shape=(pltpu.VM...  30.2 us
    pallas_call x1, Pallas kernels, local(): pl.pallas_call(last_pass, out_shape=jax.ShapeDtypeStruct((CELLS, K), BF16...  5.75 us

profile of v3, /device:TPU:6, one launch (start us, length us, event | category | flops | bytes accessed | tf_op | source)
XLA Modules:
  0.0 36.6 jit_solution(7431868753162046301)
XLA Ops:
  0.7 30.2 %shard_map.64 = (f32[16384,128]{1,0:T(8,128)S(1)}, bf16[16384,384]{1,0:T(8,128)(2,1)S(1)}, bf16[384,256]{1,0:T(8,128)(2,1)S(1)}, f32[3,64,8,128]{3,2,1,0:T(8,128)S(1)}) custom-call(bf16[16384,128]{1,0:T(8,128)(2,1)} %bitcast.6, s32[1,512]{1,0:T(1,128)} %bitcast.7, f32[1,512]{1,0:T(1,128)} %bitcast.8, f32[1,512]{1,0:T(1,128)} %bitcast.9, ...), custom_call_target="tpu_custom_call" | custom-call | tf_op jit(solution)/shard_map/pallas_call | solution.py:448
  30.9 5.7 %shard_map.65 = bf16[16384,128]{1,0:T(8,128)(2,1)} custom-call(f32[16384,128]{1,0:T(8,128)S(1)} %get-tuple-element.9.acc, bf16[16384,384]{1,0:T(8,128)(2,1)S(1)} %get-tuple-element.10.scaled, bf16[384,256]{1,0:T(8,128)(2,1)S(1)} %get-tuple-element.11.sides_w, f32[3,64,8,128]{3,2,1,0:T(8,128)S(1)} %get-tuple-element.12.bx_tab), custom_call_target="tpu_custom_call" | custom-call | tf_op jit(solution)/shard_map/pallas_call | solution.py:506

commit v4 on v3

--- a/solution.py
+++ b/solution.py
@@ -55,7 +55,7 @@
 
 
 def last_pass(acc, scaled, sides_w, bx_tab, out, result, out_sem):
-    size = 16 * TY
+    size = 8 * TY
     copies = [
         pltpu.make_async_copy(
             result.at[pl.ds(c * size, size), :], out.at[pl.ds(c * size, size), :], out_sem.at[c]
@@ -322,12 +322,12 @@
             scaled[at, :K] = (piece * low).astype(BF16)
             scaled[at, K : 2 * K] = (piece * middle).astype(BF16)
             scaled[at, 2 * K :] = (piece * top).astype(BF16)
+            s_own[at, :] = (piece * by_line(bx_tab, 1, line, middle)).astype(BF16)
             u_side[at, :] = by_line(bx_tab, 1, line, piece).astype(BF16)
-            s_own[at, :] = (piece * by_line(bx_tab, 1, line, middle)).astype(BF16)
         return 0
 
     steps = 2 * TX // lines
-    lax.fori_loop(0, steps // 2, prepare, 0, unroll=2)
+    lax.fori_loop(0, steps // 2, prepare, 0, unroll=True)
 
     for copy in ring:
         copy.wait_recv()
@@ -349,7 +349,7 @@
     gy_in = [(south, gy_out[0][1]), (north, gy_out[1][1])]
     for_sides(gy_out, lambda copy: copy.start())
 
-    lax.fori_loop(steps // 2, steps, prepare, 0, unroll=2)
+    lax.fori_loop(steps // 2, steps, prepare, 0, unroll=True)
 
     for_sides(gy_in, lambda copy: copy.wait_recv())
     total = gram[4] + gram_x[0, 1] + gram_x[1, 1] + gram_y[0] + gram_y[1]
@@ -401,7 +401,7 @@
         acc[rows, :] = acc[rows, :] + mm(s_own[rows, :], w_all[1, 1])
         return 0
 
-    lax.fori_loop(0, CELLS // size, own, 0, unroll=2)
+    lax.fori_loop(0, CELLS // size, own, 0, unroll=True)
 
     for_sides(wy_in, lambda copy: copy.wait_recv())
     wc_out = []
@@ -423,7 +423,7 @@
             acc[at, :] = acc[at, :] + (low * product[cut, :K] + top * product[cut, K:])
         return 0
 
-    lax.fori_loop(0, CELLS // size, along_gy, 0, unroll=2)
+    lax.fori_loop(0, CELLS // size, along_gy, 0, unroll=True)
 
     for_sides(wx_in, lambda copy: copy.wait_recv())
     for_sides(wc_in, lambda copy: copy.wait_recv())
@@ -508,7 +508,7 @@
         out_shape=jax.ShapeDtypeStruct((CELLS, K), BF16),
         in_specs=[vmem] * 4,
         out_specs=pl.BlockSpec(memory_space=pltpu.HBM),
-        scratch_shapes=[pltpu.VMEM((CELLS, K), BF16), dma((CELLS // (16 * TY),))],
+        scratch_shapes=[pltpu.VMEM((CELLS, K), BF16), dma((CELLS // (8 * TY),))],
         compiler_params=pltpu.CompilerParams(vmem_limit_bytes=16 * 1024 * 1024),
     )(*parts)
     return result.reshape(levels, tile_x, tile_y, members)

time: 36.7 us -> 35.8 us (0.975)
  Pallas kernels: 36 us -> 35.1 us
    pallas_call x1, Pallas kernels: 30.2 us -> 29.5 us  [local(): pl.pallas_call(functools.partial(kernel, n_gx, n_gy), out_shape=(pltpu.VM...]
where the time goes in v4:
time: 35.8 us; the launch traced here: 35.7 us
  Pallas kernels  35.1 us (98%)
  between operations  0.66 us (2%)
    pallas_call x1, Pallas kernels, local(): pl.pallas_call(functools.partial(kernel, n_gx, n_gy), out_shape=(pltpu.VM...  29.5 us
    pallas_call x1, Pallas kernels, local(): pl.pallas_call(last_pass, out_shape=jax.ShapeDtypeStruct((CELLS, K), BF16...  5.59 us

profile of v4, /device:TPU:6, one launch (start us, length us, event | category | flops | bytes accessed | tf_op | source)
XLA Modules:
  0.0 35.7 jit_solution(1690775835692571007)
XLA Ops:
  0.7 29.5 %shard_map.64 = (f32[16384,128]{1,0:T(8,128)S(1)}, bf16[16384,384]{1,0:T(8,128)(2,1)S(1)}, bf16[384,256]{1,0:T(8,128)(2,1)S(1)}, f32[3,64,8,128]{3,2,1,0:T(8,128)S(1)}) custom-call(bf16[16384,128]{1,0:T(8,128)(2,1)} %bitcast.6, s32[1,512]{1,0:T(1,128)} %bitcast.7, f32[1,512]{1,0:T(1,128)} %bitcast.8, f32[1,512]{1,0:T(1,128)} %bitcast.9, ...), custom_call_target="tpu_custom_call" | custom-call | tf_op jit(solution)/shard_map/pallas_call | solution.py:448
  30.1 5.6 %shard_map.65 = bf16[16384,128]{1,0:T(8,128)(2,1)} custom-call(f32[16384,128]{1,0:T(8,128)S(1)} %get-tuple-element.9.acc, bf16[16384,384]{1,0:T(8,128)(2,1)S(1)} %get-tuple-element.10.scaled, bf16[384,256]{1,0:T(8,128)(2,1)S(1)} %get-tuple-element.11.sides_w, f32[3,64,8,128]{3,2,1,0:T(8,128)S(1)} %get-tuple-element.12.bx_tab), custom_call_target="tpu_custom_call" | custom-call | tf_op jit(solution)/shard_map/pallas_call | solution.py:506

commit v5 on v4

--- a/solution.py
+++ b/solution.py
@@ -40,6 +40,25 @@
         jnp.concatenate([a_top, a_rest, a_top], axis=1),
         jnp.concatenate([b_top, b_top, b_rest], axis=0),
     )
+
+
+def full_sum(x):
+    return jnp.sum(jnp.sum(x, axis=0, keepdims=True), axis=1, keepdims=True)
+
+
+def times(a, b):
+    out = [None] * (len(a) + len(b) - 1)
+    for i, x in enumerate(a):
+        for j, y in enumerate(b):
+            out[i + j] = x * y if out[i + j] is None else out[i + j] + x * y
+    return out
+
+
+def combine(coefficients, powers):
+    total = coefficients[0] * powers[0]
+    for coefficient, power in zip(coefficients[1:], powers[1:]):
+        total = total + coefficient * power
+    return total
 
 
 def beta(position, has_low, has_high):
@@ -175,6 +194,10 @@
         (east, (gx + 1, gy)),
         (south, (gx, gy - 1)),
         (north, (gx, gy + 1)),
+        (jnp.logical_and(west, south), (gx - 1, gy - 1)),
+        (jnp.logical_and(west, north), (gx - 1, gy + 1)),
+        (jnp.logical_and(east, south), (gx + 1, gy - 1)),
+        (jnp.logical_and(east, north), (gx + 1, gy + 1)),
     ]
 
     barrier = pltpu.get_barrier_semaphore()
@@ -260,10 +283,7 @@
         barrier,
         BLOCK - 1
         + planes - 1
-        + west.astype(jnp.int32)
-        + east.astype(jnp.int32)
-        + south.astype(jnp.int32)
-        + north.astype(jnp.int32),
+        + sum(there.astype(jnp.int32) for there, _ in sides),
     )
 
     def remote(src, dst, send, recv, peer):
@@ -281,29 +301,31 @@
     rhs[:, :K] = perturb
     d_rows = jnp.broadcast_to(innovation, (K, OBS)).T
     rhs[:, K:] = d_rows.astype(BF16)
-    for t in range(9):
+    def for_sides(pairs, act):
+        for there, copy in pairs:
+
+            @pl.when(there)
+            def _(copy=copy):
+                act(copy)
+
+    gx_out = []
+    gx_in = []
+    for q in (0, 2, 1):
+        to_e = remote(gram.at[q], gram_x.at[0, q], send_gx.at[0, q], recv_gx.at[0, q], (gx + 1, gy))
+        to_w = remote(gram.at[6 + q], gram_x.at[1, q], send_gx.at[1, q], recv_gx.at[1, q], (gx - 1, gy))
+        gx_out += [(east, to_e), (west, to_w)]
+        gx_in += [(west, to_e), (east, to_w)]
+
+    right = rhs[...]
+    for n, t in enumerate((0, 6, 2, 8, 1, 7, 3, 5, 4)):
         weighted[t * K : (t + 1) * K, :] = (perturb_t * effective[t : t + 1, :]).astype(BF16)
-    right = rhs[...]
-    for t in range(9):
         product = mm(weighted[t * K : (t + 1) * K, :], right)
         gram[t, :K, :] = product[:, :K]
         gram[t, K:, :] = jnp.broadcast_to(
             jnp.sum(product[:, K:] * eye, axis=0, keepdims=True), (GROWS - K, K)
         )
-
-    def for_sides(pairs, act):
-        for there, copy in pairs:
-
-            @pl.when(there)
-            def _(copy=copy):
-                act(copy)
-
-    gx_out = [
-        (east, remote(gram.at[pl.ds(0, 3)], gram_x.at[0], send_gx.at[0], recv_gx.at[0], (gx + 1, gy))),
-        (west, remote(gram.at[pl.ds(6, 3)], gram_x.at[1], send_gx.at[1], recv_gx.at[1], (gx - 1, gy))),
-    ]
-    gx_in = [(west, gx_out[0][1]), (east, gx_out[1][1])]
-    for_sides(gx_out, lambda copy: copy.start())
+        if n < 6 and n % 2 == 1:
+            for_sides(gx_out[n - 1 : n + 1], lambda copy: copy.start())
 
     lines = 8
 
@@ -339,22 +361,31 @@
     for copy in cross:
         copy.start()
 
-    for_sides(gx_in, lambda copy: copy.wait_recv())
-    half[0] = gram[3] + gram_x[0, 0] + gram_x[1, 0]
-    half[1] = gram[5] + gram_x[0, 2] + gram_x[1, 2]
     gy_out = [
         (north, remote(half.at[0], gram_y.at[0], send_gy.at[0], recv_gy.at[0], (gx, gy + 1))),
         (south, remote(half.at[1], gram_y.at[1], send_gy.at[1], recv_gy.at[1], (gx, gy - 1))),
     ]
     gy_in = [(south, gy_out[0][1]), (north, gy_out[1][1])]
-    for_sides(gy_out, lambda copy: copy.start())
+    for n, q in enumerate((0, 2)):
+        for_sides(gx_in[2 * n : 2 * n + 2], lambda copy: copy.wait_recv())
+        half[n] = gram[3 + q] + gram_x[0, q] + gram_x[1, q]
+        for_sides(gy_out[n : n + 1], lambda copy: copy.start())
 
     lax.fori_loop(steps // 2, steps, prepare, 0, unroll=True)
 
-    for_sides(gy_in, lambda copy: copy.wait_recv())
+    for_sides(gx_in[4:] + gy_in, lambda copy: copy.wait_recv())
     total = gram[4] + gram_x[0, 1] + gram_x[1, 1] + gram_y[0] + gram_y[1]
     projected = jnp.broadcast_to(total[K : K + 1], (K, K)).T
-    total = total[:K]
+    total = total[:K] / (K - 1)
+    square = full_sum(total * total)
+    trace = full_sum(total * eye)
+    size_g = jnp.maximum(jnp.sqrt(square), 1e-20)
+    p1 = total / size_g
+    p2 = product3(p1, p1)
+    both = product3(p2, jnp.concatenate([p1, p2], axis=1))
+    p3, p4 = both[:, :K], both[:, K:]
+    p5 = product3(p2, p3)
+    powers = (eye, p1, p2, p3, p4, p5)
 
     for copy in cross:
         copy.wait_recv()
@@ -363,13 +394,19 @@
     denominator = jnp.sum(jnp.where(lanes < K // 2, 0.0, sums), axis=1, keepdims=True)
     inflation = numerator / denominator
 
-    system = eye / inflation + total / (K - 1)
-    frob = jnp.sqrt(jnp.sum(jnp.sum(system * system, axis=0, keepdims=True), axis=1, keepdims=True))
-    root = system / frob
-    correction = 1.5 * eye - 0.5 * root
-    root = product3(correction, root)
-    inv_root = correction
-    for sweep in range(1, NSTEPS - 1):
+    shrink = 1.0 / inflation
+    frob = jnp.sqrt(K * shrink * shrink + 2.0 * shrink * trace + square)
+    root_c = [shrink / frob, size_g / frob]
+    inv_c = None
+    for sweep in range(2):
+        joint_c = root_c if sweep == 0 else times(inv_c, root_c)
+        step_c = [-0.5 * x for x in joint_c]
+        step_c[0] = step_c[0] + 1.5
+        inv_c = step_c if sweep == 0 else times(step_c, inv_c)
+        root_c = times(root_c, step_c)
+    root = combine(root_c, powers)
+    inv_root = combine(inv_c, powers)
+    for sweep in range(2, NSTEPS - 1):
         correction = 1.5 * eye - 0.5 * product3(inv_root, root)
         both = product3(correction, jnp.concatenate([root, inv_root], axis=1))
         root, inv_root = both[:, :K], both[:, K:]
@@ -393,6 +430,15 @@
     wx_in = [(west, wx_out[0][1]), (east, wx_out[1][1])]
     for_sides(wy_out, lambda copy: copy.start())
     for_sides(wx_out, lambda copy: copy.start())
+    wc_out = []
+    wc_in = []
+    for n, (up, down, q) in enumerate(((north, south, 0), (south, north, 2))):
+        row = gy + 1 if q == 0 else gy - 1
+        to_e = remote(mine, w_all.at[0, q], send_wc.at[0, n], recv_wc.at[0, n], (gx + 1, row))
+        to_w = remote(mine, w_all.at[2, q], send_wc.at[1, n], recv_wc.at[1, n], (gx - 1, row))
+        wc_out += [(jnp.logical_and(up, east), to_e), (jnp.logical_and(up, west), to_w)]
+        wc_in += [(jnp.logical_and(down, west), to_e), (jnp.logical_and(down, east), to_w)]
+    for_sides(wc_out, lambda copy: copy.start())
 
     size = 16 * TY
 
@@ -404,14 +450,6 @@
     lax.fori_loop(0, CELLS // size, own, 0, unroll=True)
 
     for_sides(wy_in, lambda copy: copy.wait_recv())
-    wc_out = []
-    wc_in = []
-    for n, (from_y, q) in enumerate(((south, 0), (north, 2))):
-        to_e = remote(w_all.at[1, q], w_all.at[0, q], send_wc.at[0, n], recv_wc.at[0, n], (gx + 1, gy))
-        to_w = remote(w_all.at[1, q], w_all.at[2, q], send_wc.at[1, n], recv_wc.at[1, n], (gx - 1, gy))
-        wc_out += [(jnp.logical_and(from_y, east), to_e), (jnp.logical_and(from_y, west), to_w)]
-        wc_in += [(jnp.logical_and(from_y, west), to_e), (jnp.logical_and(from_y, east), to_w)]
-    for_sides(wc_out, lambda copy: copy.start())
 
     def along_gy(c, _):
         rows = pl.ds(pl.multiple_of(c * size, size), size)
@@ -481,8 +519,8 @@
             dma((BLOCK,)),
             dma((planes,)),
             dma((planes,)),
-            dma((2,)),
-            dma((2,)),
+            dma((2, 3)),
+            dma((2, 3)),
             dma((2,)),
             dma((2,)),
             dma((2,)),

time: 35.8 us -> 35.3 us (0.986)
  Pallas kernels: 35.1 us -> 34.6 us
    pallas_call x1, Pallas kernels: 29.5 us -> 29 us  [local(): pl.pallas_call(functools.partial(kernel, n_gx, n_gy), out_shape=(pltpu.VM...]
where the time goes in v5:
time: 35.3 us
  Pallas kernels  34.6 us (98%)
  between operations  0.66 us (2%)
    pallas_call x1, Pallas kernels, local(): pl.pallas_call(functools.partial(kernel, n_gx, n_gy), out_shape=(pltpu.VM...  29 us
    pallas_call x1, Pallas kernels, local(): pl.pallas_call(last_pass, out_shape=jax.ShapeDtypeStruct((CELLS, K), BF16...  5.59 us

profile of v5, /device:TPU:6, one launch (start us, length us, event | category | flops | bytes accessed | tf_op | source)
XLA Modules:
  0.0 35.3 jit_solution(13183735714701607168)
XLA Ops:
  0.7 29.0 %shard_map.64 = (f32[16384,128]{1,0:T(8,128)S(1)}, bf16[16384,384]{1,0:T(8,128)(2,1)S(1)}, bf16[384,256]{1,0:T(8,128)(2,1)S(1)}, f32[3,64,8,128]{3,2,1,0:T(8,128)S(1)}) custom-call(bf16[16384,128]{1,0:T(8,128)(2,1)} %bitcast.6, s32[1,512]{1,0:T(1,128)} %bitcast.7, f32[1,512]{1,0:T(1,128)} %bitcast.8, f32[1,512]{1,0:T(1,128)} %bitcast.9, ...), custom_call_target="tpu_custom_call" | custom-call | tf_op jit(solution)/shard_map/pallas_call | solution.py:486
  29.7 5.6 %shard_map.65 = bf16[16384,128]{1,0:T(8,128)(2,1)} custom-call(f32[16384,128]{1,0:T(8,128)S(1)} %get-tuple-element.9.acc, bf16[16384,384]{1,0:T(8,128)(2,1)S(1)} %get-tuple-element.10.scaled, bf16[384,256]{1,0:T(8,128)(2,1)S(1)} %get-tuple-element.11.sides_w, f32[3,64,8,128]{3,2,1,0:T(8,128)S(1)} %get-tuple-element.12.bx_tab), custom_call_target="tpu_custom_call" | custom-call | tf_op jit(solution)/shard_map/pallas_call | solution.py:544
